TPU v7x, 128 devices: a whole 4x4x4 slice. The times are simulated.
128 devices in a mesh: row: 8 (over y, x_hi), col: 16 (over z, x_lo, core).
Axes of the slice: x: 4 (x_hi: 2, x_lo: 2; x = x_hi * 2 + x_lo), y: 4, z: 4, core: 2. Of those that a mesh axis runs over, the one named last changes fastest.
Arguments:
- queries: bfloat16 [16384, 1024], P(('row', 'col')), may hold values from -64 to 64
- key_states: bfloat16 [16384, 128], P(('col', 'row')), may hold values from -6 to 6
- value_states: bfloat16 [16384, 128], P(('col', 'row')), may hold values from -6 to 6
- out_grad: bfloat16 [16384, 1024], P(('row', 'col')), may hold values from -6 to 6
- block_order: int32 [256], replicated, may hold values from 0 to 255, each once
Outputs:
- query_grad: bfloat16 [16384, 1024], P(('row', 'col'))
- key_grad: bfloat16 [16384, 128], P(('col', 'row'))
- value_grad: bfloat16 [16384, 128], P(('col', 'row'))
Inputs may be any that keep to these rules, and one draw needn't show every extreme that they name: `block_order`: a permutation of 0 to 255.
All inputs are finite; a program needn't handle non-finite values.
Results may differ from a plain program's by a relative error of at most 0.0055.
Values may be sent and summed in bfloat16 or wider, within the bound.
A program may use at most 192 MiB of HBM per device.

v0:
```python
import math

import jax
import jax.numpy as jnp
from jax import lax
from jax.sharding import PartitionSpec as P

H = 8
HD = 128
BLK = 64


def positions(token_index, block_order):
    block_index = token_index // BLK
    offset = token_index % BLK
    block_ids = jnp.arange(block_order.shape[0], dtype=jnp.int32)
    matches = block_index[:, None] == block_ids[None, :]
    start = jnp.sum(jnp.where(matches, block_order[None, :], 0), axis=1)
    return start * BLK + offset


def split_amount(amount, target):
    blocks = max(1, amount // target)
    for option in range(blocks, 0, -1):
        return option
    return 1


def tile_scores(query_blk, query_pos, key_blk, key_pos, scaling):
    scores = (
        jnp.einsum("ihd,jd->hij", query_blk, key_blk, preferred_element_type=jnp.float32) * scaling
    )
    visible = (key_pos[None, :] <= query_pos[:, None])[None]
    return (jnp.where(visible, scores, -1e30), visible)


def tile_visible(query_pos, key_pos):
    return (key_pos[None, :] <= query_pos[:, None])[None]


def partial_stats(scores, visible, weight_grad):
    maxima = jnp.max(scores, axis=2)
    expo = jnp.where(visible, jnp.exp(scores - maxima[:, :, None]), 0.0)
    summed = jnp.sum(expo, axis=2)
    weighted = jnp.sum(expo * weight_grad, axis=2)
    return (maxima, summed, weighted)


def join_stats(former, latter):
    maxima = jnp.maximum(former[0], latter[0])
    first = jnp.exp(former[0] - maxima)
    second = jnp.exp(latter[0] - maxima)
    summed = former[1] * first + latter[1] * second
    weighted = former[2] * first + latter[2] * second
    return (maxima, summed, weighted)


def tile_weights(scores, visible, logsum):
    return jnp.where(visible, jnp.exp(scores - logsum[:, :, None]), 0.0)


def value_scores(grad_blk, value_blk):
    return jnp.einsum("ihd,jd->hij", grad_blk, value_blk, preferred_element_type=jnp.float32)


def score_grads(attn_weights, weight_grad, delta_row):
    dscore = (attn_weights * (weight_grad - delta_row[:, :, None])).astype(jnp.bfloat16)
    return (dscore, attn_weights.astype(jnp.bfloat16))


def flat_layout(queries, key_states, value_states, out_grad, block_order, scaling):
    key_all, value_all = (
        lax.all_gather(key_states, ("row", "col"), axis=0, tiled=True),
        lax.all_gather(value_states, ("row", "col"), axis=0, tiled=True),
    )
    key_total = key_all.shape[0]
    local_rows = queries.shape[0]
    row_amount = lax.axis_size("row")
    col_amount = lax.axis_size("col")
    gathered = jnp.arange(key_total, dtype=jnp.int32)
    source = gathered // local_rows
    anchor = (
        source % col_amount * row_amount + source // col_amount
    ) * local_rows + gathered % local_rows
    key_pos = positions(anchor, block_order)
    my_piece = lax.axis_index("row") * col_amount + lax.axis_index("col")
    query_pos = positions(
        my_piece * local_rows + jnp.arange(local_rows, dtype=jnp.int32), block_order
    )
    query_local = queries.reshape(local_rows, H, HD)
    grad_local = out_grad.reshape(local_rows, H, HD)
    blocks = split_amount(key_total, 1024)
    block_rows = key_total // blocks
    key_blocks = key_all.reshape(blocks, block_rows, HD)
    value_blocks = value_all.reshape(blocks, block_rows, HD)
    kpos_blocks = key_pos.reshape(blocks, block_rows)

    def stats_pass(running, pieces):
        key_blk, value_blk, pos_blk = pieces
        scores, visible = tile_scores(query_local, query_pos, key_blk, pos_blk, scaling)
        weight_grad = value_scores(grad_local, value_blk)
        return (join_stats(running, partial_stats(scores, visible, weight_grad)), scores)

    empty_rows = jnp.zeros((H, local_rows), jnp.float32)
    start_stats = (jnp.full((H, local_rows), -1e30, jnp.float32), empty_rows, empty_rows)
    (maxima, summed, weighted), stored = lax.scan(
        stats_pass, start_stats, (key_blocks, value_blocks, kpos_blocks)
    )
    logsum = maxima + jnp.log(summed)
    deltas = weighted / summed

    def grad_pass(running, pieces):
        key_blk, value_blk, pos_blk, scores = pieces
        visible = tile_visible(query_pos, pos_blk)
        attn_weights = tile_weights(scores, visible, logsum)
        weight_grad = value_scores(grad_local, value_blk)
        dscore, attn_low = score_grads(attn_weights, weight_grad, deltas)
        running = running + jnp.einsum(
            "hij,jd->ihd", dscore, key_blk, preferred_element_type=jnp.float32
        )
        key_part = jnp.einsum(
            "hij,ihd->jd", dscore, query_local, preferred_element_type=jnp.float32
        )
        value_part = jnp.einsum(
            "hij,ihd->jd", attn_low, grad_local, preferred_element_type=jnp.float32
        )
        return (running, (key_part, value_part))

    query_acc, (key_parts, value_parts) = lax.scan(
        grad_pass,
        jnp.zeros((local_rows, H, HD), jnp.float32),
        (key_blocks, value_blocks, kpos_blocks, stored),
    )
    key_parts = key_parts.reshape(key_total, HD)
    value_parts = value_parts.reshape(key_total, HD)
    key_grad, value_grad = (
        lax.psum_scatter(key_parts, ("row", "col"), scatter_dimension=0, tiled=True),
        lax.psum_scatter(value_parts, ("row", "col"), scatter_dimension=0, tiled=True),
    )
    query_grad = (query_acc * scaling).reshape(local_rows, H * HD).astype(jnp.bfloat16)
    return (query_grad, (key_grad * scaling).astype(jnp.bfloat16), value_grad.astype(jnp.bfloat16))


def local(queries, key_states, value_states, out_grad, block_order):
    scaling = 1.0 / math.sqrt(key_states.shape[1])
    return flat_layout(queries, key_states, value_states, out_grad, block_order, scaling)


def solution(mesh):
    placed = (
        P(("row", "col"), None),
        P(("col", "row"), None),
        P(("col", "row"), None),
        P(("row", "col"), None),
        P(),
    )
    return jax.shard_map(
        local,
        mesh=mesh,
        in_specs=placed,
        out_specs=(P(("row", "col"), None), P(("col", "row"), None), P(("col", "row"), None)),
        check_vma=False,
    )
```

profile of v0, /device:TPU:0, one launch (start us, length us, event | category | flops | bytes accessed | tf_op | source)
XLA Modules:
  0.0 2064.0 jit_solution(3244588348007734374)
XLA Ops:
  11.5 5.8 select_reduce_fusion
  18.4 191.6 %all-gather.3.cloned.1.call-done = bf16[16384,128]{1,0:T(8,128)(2,1)} async-done(((bf16[128,128]{1,0:T(8,128)(2,1)}), bf16[16384,128]{1,0:T(8,128)(2,1)}) %all-gather.3.cloned.1.call-update) | async-done | bytes 4194320 | tf_op jit(solution)/shard_map/all_gather | solution.py:73
  209.9 197.8 %all-gather.5.cloned.1.call-done = bf16[16384,128]{1,0:T(8,128)(2,1)} async-done(((bf16[128,128]{1,0:T(8,128)(2,1)}), bf16[16384,128]{1,0:T(8,128)(2,1)}) %all-gather.5.cloned.1.call-update) | async-done | bytes 4194320 | tf_op jit(solution)/shard_map/all_gather | solution.py:74
  407.8 171.6 %while.32 = (s32[]{:T(128)}, f32[8,128]{1,0:T(8,128)S(1)}, f32[8,128]{1,0:T(8,128)S(1)}, f32[8,128]{1,0:T(8,128)S(1)}, f32[16,8,128,1024]{2,3,1,0:T(8,128)}, /*i...) while((s32[]{:T(128)}, f32[8,128]{1,0:T(8,128)S(1)}, ...), condition=%wide.region_6.7_spmd.clone, body=%wide.region_2.6_spmd.clone.sunk | while | flops 553791488 | bytes 39545000 | solution.py:106
  579.3 167.4 %while.33 = (s32[]{:T(128)}, f32[128,8,128]{0,2,1:T(8,128)S(1)}, f32[16,1024,128]{2,1,0:T(8,128)}, f32[16,1024,128]{2,1,0:T(8,128)}, bf16[16,1024,128]{2,1,0:T(8...) while((s32[]{:T(128)}, f32[128,8,128]{0,2,1:T(8,128)S(1)}, ...), condition=%wide.region_8.9_spmd.clone, body=%wide.region_7.8_spmd.clone.sunk | while | flops 1082523648 | bytes 18509468 | solution.py:129
  579.6 3.5 fusion.114
  586.1 3.7 fusion.117
  590.0 3.5 fusion.114
  596.5 3.8 fusion.117
  600.5 3.5 fusion.114
  607.0 3.7 fusion.117
  617.5 3.7 fusion.117
  627.9 3.8 fusion.117
  631.9 3.5 fusion.114
  638.4 3.7 fusion.117
  642.4 3.5 fusion.114
  648.8 3.7 fusion.117
  652.8 3.5 fusion.114
  659.3 3.7 fusion.117
  663.2 3.5 fusion.114
  669.7 3.8 fusion.117
  680.2 3.8 fusion.117
  690.7 3.7 fusion.117
  701.2 3.7 fusion.117
  705.1 3.5 fusion.114
  711.6 3.8 fusion.117
  715.6 3.5 fusion.114
  722.1 3.7 fusion.117
  732.5 3.7 fusion.117
  743.0 3.7 fusion.117
  748.2 654.6 %reduce-scatter.5.cloned.1.call-done = f32[128,128]{1,0:T(8,128)} async-done(((f32[16384,128]{1,0:T(8,128)}), f32[128,128]{1,0:T(8,128)}) %reduce-scatter.5.cloned.1.call-update) | async-done | bytes 65552 | tf_op jit(solution)/shard_map/reduce_scatter | solution.py:138
  1404.3 651.7 %reduce-scatter.3.cloned.1.call-done = f32[128,128]{1,0:T(8,128)} async-done(((f32[16384,128]{1,0:T(8,128)}), f32[128,128]{1,0:T(8,128)}) %reduce-scatter.3.cloned.1.call-update) | async-done | bytes 65552 | tf_op jit(solution)/shard_map/reduce_scatter | solution.py:137
  (278 shorter events, 255.8 us)
Async XLA Ops:
  7.2 202.8 %all-gather.3.cloned.1.call-start = ((), (), s32[]{:S(2)}) async-start(), calls=%async_computation.2 | async-start | bytes 4227072 | tf_op jit(solution)/shard_map/all_gather | solution.py:73
  7.9 399.9 %all-gather.5.cloned.1.call-start = ((), (), s32[]{:S(2)}) async-start(), calls=%async_computation.3 | async-start | bytes 4227072 | tf_op jit(solution)/shard_map/all_gather | solution.py:74
  8.6 1394.2 %reduce-scatter.5.cloned.1.call-start = ((), (), s32[]{:S(2)}) async-start(), calls=%async_computation.5 | async-start | bytes 8454144 | tf_op jit(solution)/shard_map/reduce_scatter | solution.py:138
  409.7 3.3 copy-start
  420.4 3.2 copy-start
  431.1 3.3 copy-start
  441.8 3.3 copy-start
  452.6 3.3 copy-start
  463.3 3.2 copy-start
  474.0 3.3 copy-start
  484.7 3.3 copy-start
  495.5 3.4 copy-start
  506.4 3.2 copy-start
  517.0 3.2 copy-start
  527.7 3.2 copy-start
  538.4 3.4 copy-start
  549.2 3.2 copy-start
  559.9 3.2 copy-start
  570.6 3.2 copy-start
  746.7 1309.3 %reduce-scatter.3.cloned.1.call-start = ((), (), s32[]{:S(2)}) async-start(), calls=%async_computation.4 | async-start | bytes 8454144 | tf_op jit(solution)/shard_map/reduce_scatter | solution.py:137
Sparse Core Ops, SparseCore 0:
  9.7 200.1 all-gather.2
  211.7 196.0 all-gather.4
  746.9 655.9 reduce-scatter.4
  1405.1 650.9 reduce-scatter.2
where the time goes:
time: 2070 us; the launch traced here: 2060 us
  waiting for transfers between devices  1700 us (82%)
  matrix products  227 us (11%)
  other arithmetic  114 us (6%)
    reduce_scatter x1, waiting for transfers between devices, flat_layout(): lax.psum_scatter(value_parts, ('row', 'col'), scatter_dimension=0, tiled=...  655 us
    reduce_scatter x1, waiting for transfers between devices, flat_layout(): lax.psum_scatter(key_parts, ('row', 'col'), scatter_dimension=0, tiled=True)  652 us
    all_gather x1, waiting for transfers between devices, flat_layout(): lax.all_gather(value_states, ('row', 'col'), axis=0, tiled=True)  198 us
    all_gather x1, waiting for transfers between devices, flat_layout(): lax.all_gather(key_states, ('row', 'col'), axis=0, tiled=True)  192 us
    dot_general x32, matrix products, value_scores(): jnp.einsum('ihd,jd->hij', grad_blk, value_blk, preferred_element_type=jnp...  91.6 us
    dot_general x16, matrix products, grad_pass(): jnp.einsum('hij,ihd->jd', attn_low, grad_local, preferred_element_type=jn...  59.9 us
    reduce_sum x16, other arithmetic, partial_stats(): summed = jnp.sum(expo, axis=2)  50.9 us
    dynamic_update_slice x16, other arithmetic, flat_layout(): lax.scan(stats_pass, start_stats, (key_blocks, value_blocks, kpos_blocks))  46.5 us
  transfers between devices with their start and end apart: 4, of which 4 were waited for; matrix products, arithmetic and copies ran while one was open for 1% of the time, Pallas kernels for 0%

commit v1 on v0

v1 whole, which is shorter than its diff:
```python
import math

import jax
import jax.numpy as jnp
from jax import lax
from jax.sharding import PartitionSpec as P

H = 8
HD = 128
BLK = 64


def positions(token_index, block_order):
    return block_order[token_index // BLK] * BLK + token_index % BLK


def partial_stats(scores, visible, weight_grad):
    maxima = jnp.max(scores, axis=1)
    expo = jnp.where(visible, jnp.exp(scores - maxima[:, None]), 0.0)
    summed = jnp.sum(expo, axis=1)
    weighted = jnp.sum(expo * weight_grad, axis=1)
    return (maxima, summed, weighted)


def join_stats(former, latter):
    maxima = jnp.maximum(former[0], latter[0])
    first = jnp.exp(former[0] - maxima)
    second = jnp.exp(latter[0] - maxima)
    summed = former[1] * first + latter[1] * second
    weighted = former[2] * first + latter[2] * second
    return (maxima, summed, weighted)


def tile_grid(queries, key_states, value_states, out_grad, block_order, scaling):
    row_amount = lax.axis_size("row")
    col_amount = lax.axis_size("col")
    r = lax.axis_index("row")
    c = lax.axis_index("col")
    local_rows = queries.shape[0]
    query_all = lax.all_gather(queries, "row", axis=0, tiled=True)
    grad_all = lax.all_gather(out_grad, "row", axis=0, tiled=True)
    key_all = lax.all_gather(key_states, "col", axis=0, tiled=True)
    value_all = lax.all_gather(value_states, "col", axis=0, tiled=True)
    q_total = query_all.shape[0]
    k_total = key_all.shape[0]

    qi = jnp.arange(q_total, dtype=jnp.int32)
    q_anchor = ((qi // local_rows) * col_amount + c) * local_rows + qi % local_rows
    query_pos = positions(q_anchor, block_order)
    ki = jnp.arange(k_total, dtype=jnp.int32)
    k_anchor = ((ki // local_rows) * row_amount + r) * local_rows + ki % local_rows
    key_pos = positions(k_anchor, block_order)

    qf = query_all.reshape(q_total * H, HD)
    gf = grad_all.reshape(q_total * H, HD)
    rpos = jnp.repeat(query_pos, H)

    blocks = 2
    block_rows = k_total // blocks
    key_blocks = key_all.reshape(blocks, block_rows, HD)
    value_blocks = value_all.reshape(blocks, block_rows, HD)
    kpos_blocks = key_pos.reshape(blocks, block_rows)

    def scores_of(key_blk, pos_blk):
        s = jnp.dot(qf, key_blk.T, preferred_element_type=jnp.float32) * scaling
        visible = pos_blk[None, :] <= rpos[:, None]
        return jnp.where(visible, s, -1e30), visible

    def stats_pass(running, pieces):
        key_blk, value_blk, pos_blk = pieces
        s, visible = scores_of(key_blk, pos_blk)
        dp = jnp.dot(gf, value_blk.T, preferred_element_type=jnp.float32)
        return (join_stats(running, partial_stats(s, visible, dp)), None)

    rows = q_total * H
    empty = jnp.zeros((rows,), jnp.float32)
    start = (jnp.full((rows,), -1e30, jnp.float32), empty, empty)
    (maxima, summed, weighted), _ = lax.scan(
        stats_pass, start, (key_blocks, value_blocks, kpos_blocks)
    )
    top = lax.pmax(maxima, "row")
    factor = jnp.exp(maxima - top)
    summed, weighted = lax.psum((summed * factor, weighted * factor), "row")
    logsum = top + jnp.log(summed)
    deltas = weighted / summed

    def grad_pass(running, pieces):
        key_blk, value_blk, pos_blk = pieces
        s, visible = scores_of(key_blk, pos_blk)
        attn = jnp.where(visible, jnp.exp(s - logsum[:, None]), 0.0)
        dp = jnp.dot(gf, value_blk.T, preferred_element_type=jnp.float32)
        dscore = (attn * (dp - deltas[:, None])).astype(jnp.bfloat16)
        attn_low = attn.astype(jnp.bfloat16)
        running = running + jnp.dot(dscore, key_blk, preferred_element_type=jnp.float32)
        key_part = jnp.dot(dscore.T, qf, preferred_element_type=jnp.float32)
        value_part = jnp.dot(attn_low.T, gf, preferred_element_type=jnp.float32)
        return (running, (key_part, value_part))

    query_acc, (key_parts, value_parts) = lax.scan(
        grad_pass,
        jnp.zeros((rows, HD), jnp.float32),
        (key_blocks, value_blocks, kpos_blocks),
    )
    key_parts = key_parts.reshape(k_total, HD)
    value_parts = value_parts.reshape(k_total, HD)
    key_grad = lax.psum_scatter(key_parts, "col", scatter_dimension=0, tiled=True)
    value_grad = lax.psum_scatter(value_parts, "col", scatter_dimension=0, tiled=True)
    query_acc = query_acc.reshape(q_total, H * HD)
    query_grad = lax.psum_scatter(query_acc, "row", scatter_dimension=0, tiled=True)
    return (
        (query_grad * scaling).astype(jnp.bfloat16),
        (key_grad * scaling).astype(jnp.bfloat16),
        value_grad.astype(jnp.bfloat16),
    )


def local(queries, key_states, value_states, out_grad, block_order):
    scaling = 1.0 / math.sqrt(key_states.shape[1])
    return tile_grid(queries, key_states, value_states, out_grad, block_order, scaling)


def solution(mesh):
    placed = (
        P(("row", "col"), None),
        P(("col", "row"), None),
        P(("col", "row"), None),
        P(("row", "col"), None),
        P(),
    )
    return jax.shard_map(
        local,
        mesh=mesh,
        in_specs=placed,
        out_specs=(P(("row", "col"), None), P(("col", "row"), None), P(("col", "row"), None)),
        check_vma=False,
    )
```

time: 2070 us -> 705 us (0.34)
  waiting for transfers between devices: 1700 us -> 329 us
  blocking collectives: 0 us -> 84.4 us
  other arithmetic: 114 us -> 37.4 us
  local copies, waits for them, and re-layouts: 9.47 us -> 33.8 us
  matrix products: 227 us -> 204 us
    reduce_scatter x2 -> x3, waiting for transfers between devices: 1310 us -> 202 us  [the longest x1 85.5 us: tile_grid(): lax.psum_scatter(query_acc, 'row', scatter_dimension=0, tiled=True)]
    all_gather x2, waiting for transfers between devices: 389 us -> 43.5 us  [the longest x1 43.5 us: tile_grid(): grad_all = lax.all_gather(out_grad, 'row', axis=0, tiled=True)]
    psum x0 -> x1, waiting for transfers between devices: none -> 81.6 us  [tile_grid(): summed, weighted = lax.psum((summed * factor, weighted * factor), 'row')]
    dynamic_update_slice x16 -> x0, other arithmetic: 46.5 us -> none  [flat_layout(): lax.scan(stats_pass, start_stats, (key_blocks, value_blocks, kpos_blocks))]
    all_gather x0 -> x2, blocking collectives: none -> 46.3 us  [the longest x1 25.6 us: tile_grid(): key_all = lax.all_gather(key_states, 'col', axis=0, tiled=True)]
    pmax x0 -> x1, blocking collectives: none -> 38.1 us  [tile_grid(): top = lax.pmax(maxima, 'row')]
    reduce_sum x18 -> x2, other arithmetic: 57.5 us -> 30.9 us  [partial_stats(): summed = jnp.sum(expo, axis=1)]
    dot_general x96 -> x14, matrix products: 227 us -> 204 us  [the longest x4 51.8 us: scores_of(): s = jnp.dot(qf, key_blk.T, preferred_element_type=jnp.float32) * scaling]
  transfers between devices with their start and end apart: 4 -> 6, of which waited for: 4 -> 5; matrix products, arithmetic and copies ran while one was open for 1% -> 4% of each run, Pallas kernels for 0% -> 0%
where the time goes in v1:
time: 705 us; the launch traced here: 704 us
  waiting for transfers between devices  329 us (47%)
  matrix products  204 us (29%)
  blocking collectives  84.4 us (12%)
  other arithmetic  37.4 us (5%)
  local copies, waits for them, and re-layouts  33.8 us (5%)
  between operations  14.3 us (2%)
    reduce_scatter x1, waiting for transfers between devices, tile_grid(): lax.psum_scatter(query_acc, 'row', scatter_dimension=0, tiled=True)  85.5 us
    psum x1, waiting for transfers between devices, tile_grid(): summed, weighted = lax.psum((summed * factor, weighted * factor), 'row')  81.6 us
    reduce_scatter x1, waiting for transfers between devices, tile_grid(): lax.psum_scatter(key_parts, 'col', scatter_dimension=0, tiled=True)  61.9 us
    reduce_scatter x1, waiting for transfers between devices, tile_grid(): lax.psum_scatter(value_parts, 'col', scatter_dimension=0, tiled=True)  54.6 us
    dot_general x4, matrix products, scores_of(): s = jnp.dot(qf, key_blk.T, preferred_element_type=jnp.float32) * scaling  51.8 us
    all_gather x1, waiting for transfers between devices, tile_grid(): grad_all = lax.all_gather(out_grad, 'row', axis=0, tiled=True)  43.5 us
    dot_general x2, matrix products, grad_pass(): dp = jnp.dot(gf, value_blk.T, preferred_element_type=jnp.float32)  43.3 us
    pmax x1, blocking collectives, tile_grid(): top = lax.pmax(maxima, 'row')  38.1 us
  transfers between devices with their start and end apart: 6, of which 5 were waited for; matrix products, arithmetic and copies ran while one was open for 4% of the time, Pallas kernels for 0%

profile of v1, /device:TPU:0, one launch (start us, length us, event | category | flops | bytes accessed | tf_op | source)
XLA Modules:
  0.0 703.9 jit_solution(8597683246358550744)
XLA Ops:
  8.8 6.9 gather_fusion.1
  15.8 13.2 %gather_fusion = s32[2048]{0:T(1024)S(1)} fusion(s32[256]{0:T(256)S(1)} %copy-done, s32[2048]{0:T(1024)S(1)} %broadcast_clamp_fusion), kind=kCustom, calls=%fused_computation | custom fusion | bytes 24576 | tf_op jit(solution)/shard_map/gather | solution.py:14
  29.1 25.6 %all_gather.12 = bf16[2048,128]{1,0:T(8,128)(2,1)S(1)} all-gather(bf16[128,128]{1,0:T(8,128)(2,1)} %param.10), channel_id=1, replica_groups=mesh['row'=8,'col'=16] {'col'}, dimensions={0}, use_global_device_ids=true | all-gather | bytes 557056 | tf_op jit(solution)/shard_map/all_gather | solution.py:42
  54.7 20.7 %all_gather.14 = bf16[2048,128]{1,0:T(8,128)(2,1)} all-gather(bf16[128,128]{1,0:T(8,128)(2,1)} %param.11), channel_id=1, replica_groups=mesh['row'=8,'col'=16] {'col'}, dimensions={0}, use_global_device_ids=true | all-gather | bytes 557056 | tf_op jit(solution)/shard_map/all_gather | solution.py:43
  75.4 2.8 reshape.275
  78.3 43.5 %all-gather.5.cloned.1.call-done = bf16[1024,1024]{1,0:T(8,128)(2,1)} async-done(((bf16[128,1024]{1,0:T(8,128)(2,1)}), bf16[1024,1024]{1,0:T(8,128)(2,1)}) %all-gather.5.cloned.1.call-update) | async-done | bytes 2097168 | tf_op jit(solution)/shard_map/all_gather | solution.py:41
  121.7 4.2 reshape.277
  125.9 92.9 %while.30 = (s32[]{:T(128)}, f32[8192]{0:T(1024)S(1)}, f32[8192]{0:T(1024)S(1)}, f32[8192]{0:T(1024)S(1)}, s32[2,1024]{1,0:T(2,128)S(1)}, /*index=5*/bf16[2,1024...) while((s32[]{:T(128)}, f32[8192]{0:T(1024)S(1)}, ...), condition=%wide.region_4.5_spmd.clone, body=%wide.region_0.4_spmd.clone.sunk | while | flops 4437671936 | bytes 106225808 | solution.py:78
  126.4 12.7 %fusion.102 = (f32[8192]{0:T(1024)S(1)}, f32[1024,8192]{1,0:T(8,128)}) fusion(s32[8192]{0:T(1024)S(1)} %le.117, s32[1024]{0:T(1024)S(1)} %bitcast.120, bf16[8192,128]{1,0:T(8,128)(2,1)S(1)} %get-tuple-element.431, bf16[2,1024,128]{2,1,0:T(8,128)(2,1)S(1)} %get-tuple-element.430, s32[]{:T(128)S(6)} %copy.14), kind=kOutput, calls=%fused_computation.8.clone.1 | convolution fusion | flops 2181029888 | bytes 35983364 | tf_op jit(solution)/shard_map/while/body/eval_jaxpr/dot_general | solution.py:65
  139.1 17.7 %fusion.103 = f32[8192]{0:T(1024)S(1)} fusion(f32[1024,8192]{1,0:T(8,128)} %get-tuple-element.385, bf16[8192,128]{1,0:T(8,128)(2,1)} %get-tuple-element.433, f32[8192]{0:T(1024)S(1)} %get-tuple-element.386, s32[8192]{0:T(1024)S(1)} %le.117, s32[1024]{0:T(1024)S(1)} %bitcast.121, bf16[2,1024,128]{2,1,0:T(8,128)(2,1)} %get-tuple-element.432, s32[]{:T(128)S(6)} %copy.14), kind=kOutput, calls=%fused_computation.7.clone.1 | convolution fusion | flops 2206195712 | bytes 36016132 | tf_op jit(solution)/shard_map/while/body/eval_jaxpr/dot_general | solution.py:72
  156.8 15.5 %fusion.105 = f32[8192]{0:T(1024)S(1)} fusion(f32[1024,8192]{1,0:T(8,128)} %get-tuple-element.385, f32[8192]{0:T(1024)S(1)} %get-tuple-element.386, s32[8192]{0:T(1024)S(1)} %le.117, s32[1024]{0:T(1024)S(1)} %bitcast.122), kind=kLoop, calls=%fused_computation.9.clone.1 | loop fusion | flops 50323456 | bytes 33656832 | tf_op jit(solution)/shard_map/while/body/eval_jaxpr/reduce_sum | solution.py:20
  172.8 12.7 %fusion.102 = (f32[8192]{0:T(1024)S(1)}, f32[1024,8192]{1,0:T(8,128)}) fusion(s32[8192]{0:T(1024)S(1)} %le.117, s32[1024]{0:T(1024)S(1)} %bitcast.120, bf16[8192,128]{1,0:T(8,128)(2,1)S(1)} %get-tuple-element.431, bf16[2,1024,128]{2,1,0:T(8,128)(2,1)S(1)} %get-tuple-element.430, s32[]{:T(128)S(6)} %copy.14), kind=kOutput, calls=%fused_computation.8.clone.1 | convolution fusion | flops 2181029888 | bytes 35983364 | tf_op jit(solution)/shard_map/while/body/eval_jaxpr/dot_general | solution.py:65
  185.5 17.7 %fusion.103 = f32[8192]{0:T(1024)S(1)} fusion(f32[1024,8192]{1,0:T(8,128)} %get-tuple-element.385, bf16[8192,128]{1,0:T(8,128)(2,1)} %get-tuple-element.433, f32[8192]{0:T(1024)S(1)} %get-tuple-element.386, s32[8192]{0:T(1024)S(1)} %le.117, s32[1024]{0:T(1024)S(1)} %bitcast.121, bf16[2,1024,128]{2,1,0:T(8,128)(2,1)} %get-tuple-element.432, s32[]{:T(128)S(6)} %copy.14), kind=kOutput, calls=%fused_computation.7.clone.1 | convolution fusion | flops 2206195712 | bytes 36016132 | tf_op jit(solution)/shard_map/while/body/eval_jaxpr/dot_general | solution.py:72
  203.2 15.5 %fusion.105 = f32[8192]{0:T(1024)S(1)} fusion(f32[1024,8192]{1,0:T(8,128)} %get-tuple-element.385, f32[8192]{0:T(1024)S(1)} %get-tuple-element.386, s32[8192]{0:T(1024)S(1)} %le.117, s32[1024]{0:T(1024)S(1)} %bitcast.122), kind=kLoop, calls=%fused_computation.9.clone.1 | loop fusion | flops 50323456 | bytes 33656832 | tf_op jit(solution)/shard_map/while/body/eval_jaxpr/reduce_sum | solution.py:20
  218.8 38.1 %pmax.7 = f32[8192]{0:T(1024)S(1)} all-reduce(f32[8192]{0:T(1024)S(1)} %get-tuple-element.121), channel_id=1, replica_groups=mesh['row'=8,'col'=16] {'row'}, use_global_device_ids=true, to_apply=%region_5.6 | all-reduce | flops 8192 | bytes 65536 | tf_op jit(solution)/shard_map/pmax | solution.py:81
  257.6 81.6 %all-reduce.3.cloned.1.call-done = (f32[8192]{0:T(1024)}, f32[8192]{0:T(1024)}) async-done(((f32[8192]{0:T(1024)}, f32[8192]{0:T(1024)}), (f32[8192]{0:T(1024)}, f32[8192]{0:T(1024)})) %all-reduce.3.cloned.1.call-update) | async-done | bytes 65552 | tf_op jit(solution)/shard_map/psum | solution.py:83
  340.0 144.7 %while.31 = (s32[]{:T(128)}, f32[8192,128]{1,0:T(8,128)}, f32[2,1024,128]{2,1,0:T(8,128)}, f32[2,1024,128]{2,1,0:T(8,128)}, s32[2,1024]{1,0:T(2,128)S(1)}, /*ind...) while((s32[]{:T(128)}, f32[8192,128]{1,0:T(8,128)}, ...), condition=%wide.region_9.10_spmd.clone, body=%wide.region_8.9_spmd.clone.sunk | while | flops 10856955904 | bytes 180375776 | solution.py:99
  340.6 13.2 %fusion.117 = f32[1024,8192]{1,0:T(8,128)} fusion(bf16[8192,128]{1,0:T(8,128)(2,1)S(1)} %get-tuple-element.471, bf16[2,1024,128]{2,1,0:T(8,128)(2,1)S(1)} %get-tuple-element.470, s32[]{:T(128)S(6)} %copy.28), kind=kOutput, calls=%fused_computation.40.clone.1 | convolution fusion | flops 2147483648 | bytes 35913732 | tf_op jit(solution)/shard_map/while/body/eval_jaxpr/dot_general | solution.py:65
  353.8 15.1 %fusion.120 = f32[2,1024,128]{2,1,0:T(8,128)} fusion(f32[2,1024,128]{2,1,0:T(8,128)} %get-tuple-element.454, s32[]{:T(128)S(6)} %copy.28, bf16[8192,128]{1,0:T(8,128)(2,1)S(1)} %copy-done.2, f32[1024,8192]{1,0:T(8,128)} %fusion.117, f32[8192]{0:T(1024)S(1)} %get-tuple-element.472, s32[8192]{0:T(1024)S(1)} %le.124, s32[1024]{0:T(1024)S(1)} %bitcast.123), kind=kOutput, calls=%fused_computation.37.clone.1 | convolution fusion | flops 2197815296 | bytes 36245508 | tf_op jit(solution)/shard_map/while/body/eval_jaxpr/dot_general | solution.py:96
  368.9 21.6 %fusion.118 = bf16[8192,1024]{0,1:T(8,128)(2,1)} fusion(f32[1024,8192]{1,0:T(8,128)} %fusion.117, f32[8192]{0:T(1024)S(1)} %get-tuple-element.475, f32[8192]{0:T(1024)S(1)} %get-tuple-element.472, s32[8192]{0:T(1024)S(1)} %le.124, s32[1024]{0:T(1024)S(1)} %bitcast.124, bf16[8192,128]{1,0:T(8,128)(2,1)} %get-tuple-element.474, ...), kind=kOutput, calls=%fused_computation.30.clone.1 | convolution fusion | flops 2214592512 | bytes 52793348 | tf_op jit(solution)/shard_map/while/body/eval_jaxpr/dot_general | solution.py:91
  390.5 8.9 %fusion.119 = f32[2,1024,128]{2,1,0:T(8,128)} fusion(f32[2,1024,128]{2,1,0:T(8,128)} %get-tuple-element.453, s32[]{:T(128)S(6)} %copy.28, bf16[8192,1024]{0,1:T(8,128)(2,1)} %fusion.118, bf16[8192,128]{1,0:T(8,128)(2,1)S(1)} %get-tuple-element.471), kind=kOutput, calls=%fused_computation.35.clone.1 | convolution fusion | flops 2147483648 | bytes 19398660 | tf_op jit(solution)/shard_map/while/body/eval_jaxpr/dot_general | solution.py:95
  399.5 12.4 %convolution_add_fusion.2 = f32[8192,128]{1,0:T(8,128)} fusion(bf16[8192,1024]{0,1:T(8,128)(2,1)} %fusion.118, f32[8192,128]{1,0:T(8,128)} %get-tuple-element.452, pred[]{:T(512)S(6)} %compare.43, bf16[2,1024,128]{2,1,0:T(8,128)(2,1)S(1)} %get-tuple-element.470, s32[]{:T(128)S(6)} %copy.28), kind=kOutput, calls=%fused_computation.33.clone.1 | convolution fusion | flops 2149580800 | bytes 25427972 | tf_op jit(solution)/shard_map/while/body/eval_jaxpr/dot_general | solution.py:94
  412.3 13.2 %fusion.117 = f32[1024,8192]{1,0:T(8,128)} fusion(bf16[8192,128]{1,0:T(8,128)(2,1)S(1)} %get-tuple-element.471, bf16[2,1024,128]{2,1,0:T(8,128)(2,1)S(1)} %get-tuple-element.470, s32[]{:T(128)S(6)} %copy.28), kind=kOutput, calls=%fused_computation.40.clone.1 | convolution fusion | flops 2147483648 | bytes 35913732 | tf_op jit(solution)/shard_map/while/body/eval_jaxpr/dot_general | solution.py:65
  425.5 15.1 %fusion.120 = f32[2,1024,128]{2,1,0:T(8,128)} fusion(f32[2,1024,128]{2,1,0:T(8,128)} %get-tuple-element.454, s32[]{:T(128)S(6)} %copy.28, bf16[8192,128]{1,0:T(8,128)(2,1)S(1)} %copy-done.2, f32[1024,8192]{1,0:T(8,128)} %fusion.117, f32[8192]{0:T(1024)S(1)} %get-tuple-element.472, s32[8192]{0:T(1024)S(1)} %le.124, s32[1024]{0:T(1024)S(1)} %bitcast.123), kind=kOutput, calls=%fused_computation.37.clone.1 | convolution fusion | flops 2197815296 | bytes 36245508 | tf_op jit(solution)/shard_map/while/body/eval_jaxpr/dot_general | solution.py:96
  440.6 21.6 %fusion.118 = bf16[8192,1024]{0,1:T(8,128)(2,1)} fusion(f32[1024,8192]{1,0:T(8,128)} %fusion.117, f32[8192]{0:T(1024)S(1)} %get-tuple-element.475, f32[8192]{0:T(1024)S(1)} %get-tuple-element.472, s32[8192]{0:T(1024)S(1)} %le.124, s32[1024]{0:T(1024)S(1)} %bitcast.124, bf16[8192,128]{1,0:T(8,128)(2,1)} %get-tuple-element.474, ...), kind=kOutput, calls=%fused_computation.30.clone.1 | convolution fusion | flops 2214592512 | bytes 52793348 | tf_op jit(solution)/shard_map/while/body/eval_jaxpr/dot_general | solution.py:91
  462.2 8.9 %fusion.119 = f32[2,1024,128]{2,1,0:T(8,128)} fusion(f32[2,1024,128]{2,1,0:T(8,128)} %get-tuple-element.453, s32[]{:T(128)S(6)} %copy.28, bf16[8192,1024]{0,1:T(8,128)(2,1)} %fusion.118, bf16[8192,128]{1,0:T(8,128)(2,1)S(1)} %get-tuple-element.471), kind=kOutput, calls=%fused_computation.35.clone.1 | convolution fusion | flops 2147483648 | bytes 19398660 | tf_op jit(solution)/shard_map/while/body/eval_jaxpr/dot_general | solution.py:95
  471.1 13.6 %convolution_add_fusion.2 = f32[8192,128]{1,0:T(8,128)} fusion(bf16[8192,1024]{0,1:T(8,128)(2,1)} %fusion.118, f32[8192,128]{1,0:T(8,128)} %get-tuple-element.452, pred[]{:T(512)S(6)} %compare.43, bf16[2,1024,128]{2,1,0:T(8,128)(2,1)S(1)} %get-tuple-element.470, s32[]{:T(128)S(6)} %copy.28), kind=kOutput, calls=%fused_computation.33.clone.1 | convolution fusion | flops 2149580800 | bytes 25427972 | tf_op jit(solution)/shard_map/while/body/eval_jaxpr/dot_general | solution.py:94
  485.4 4.9 reshape.278
  490.3 54.6 %reduce-scatter.8.cloned.1.call-done = f32[128,128]{1,0:T(8,128)} async-done(((f32[2048,128]{1,0:T(8,128)}), f32[128,128]{1,0:T(8,128)}) %reduce-scatter.8.cloned.1.call-update) | async-done | bytes 65552 | tf_op jit(solution)/shard_map/reduce_scatter | solution.py:107
  546.4 61.9 %reduce-scatter.6.cloned.1.call-done = f32[128,128]{1,0:T(8,128)} async-done(((f32[2048,128]{1,0:T(8,128)}), f32[128,128]{1,0:T(8,128)}) %reduce-scatter.6.cloned.1.call-update) | async-done | bytes 65552 | tf_op jit(solution)/shard_map/reduce_scatter | solution.py:106
  609.7 85.5 %reduce-scatter.4.cloned.1.call-done = f32[128,1024]{1,0:T(8,128)} async-done(((f32[1024,1024]{1,0:T(8,128)}), f32[128,1024]{1,0:T(8,128)}) %reduce-scatter.4.cloned.1.call-update) | async-done | bytes 524304 | tf_op jit(solution)/shard_map/reduce_scatter | solution.py:109
  695.3 1.8 multiply_convert_fusion
  (61 shorter events, 8.7 us)
Async XLA Ops:
  7.2 1.6 copy-start
  7.2 68.3 %all-gather.3.cloned.1.call-start = ((), (), s32[]{:S(2)}) async-start(), calls=%async_computation.3 | async-start | bytes 2359296 | tf_op jit(solution)/shard_map/all_gather | solution.py:40
  7.9 113.8 %all-gather.5.cloned.1.call-start = ((), (), s32[]{:S(2)}) async-start(), calls=%async_computation.4 | async-start | bytes 2359296 | tf_op jit(solution)/shard_map/all_gather | solution.py:41
  8.7 330.5 %all-reduce.3.cloned.1.call-start = ((), (), s32[]{:S(2)}) async-start(), calls=%async_computation.8 | async-start | bytes 131072 | tf_op jit(solution)/shard_map/psum | solution.py:83
  257.5 287.4 %reduce-scatter.8.cloned.1.call-start = ((), (), s32[]{:S(2)}) async-start(), calls=%async_computation.7 | async-start | bytes 1114112 | tf_op jit(solution)/shard_map/reduce_scatter | solution.py:107
  340.6 13.2 %copy-start.2 = (bf16[8192,128]{1,0:T(8,128)(2,1)S(1)}, bf16[8192,128]{1,0:T(8,128)(2,1)}, u32[]{:S(2)}) copy-start(bf16[8192,128]{1,0:T(8,128)(2,1)} %get-tuple-element.474) | copy-start | bytes 6291460 | tf_op jit(solution)/shard_map/while
  353.8 15.1 %copy-start.3 = (bf16[2,1024,128]{2,1,0:T(8,128)(2,1)S(1)}, bf16[2,1024,128]{2,1,0:T(8,128)(2,1)}, u32[]{:S(2)}) copy-start(bf16[2,1024,128]{2,1,0:T(8,128)(2,1)} %get-tuple-element.473) | copy-start | bytes 1572868 | tf_op jit(solution)/shard_map/while
  412.3 13.2 %copy-start.2 = (bf16[8192,128]{1,0:T(8,128)(2,1)S(1)}, bf16[8192,128]{1,0:T(8,128)(2,1)}, u32[]{:S(2)}) copy-start(bf16[8192,128]{1,0:T(8,128)(2,1)} %get-tuple-element.474) | copy-start | bytes 6291460 | tf_op jit(solution)/shard_map/while
  425.5 15.1 %copy-start.3 = (bf16[2,1024,128]{2,1,0:T(8,128)(2,1)S(1)}, bf16[2,1024,128]{2,1,0:T(8,128)(2,1)}, u32[]{:S(2)}) copy-start(bf16[2,1024,128]{2,1,0:T(8,128)(2,1)} %get-tuple-element.473) | copy-start | bytes 1572868 | tf_op jit(solution)/shard_map/while
  484.7 212.4 %copy-start.1 = (s32[256]{0:T(256)S(1)}, s32[256]{0:T(256)}, u32[]{:S(2)}) copy-start(s32[256]{0:T(256)} %param.13) | copy-start | bytes 3076
  484.7 123.5 %reduce-scatter.6.cloned.1.call-start = ((), (), s32[]{:S(2)}) async-start(), calls=%async_computation.6 | async-start | bytes 1114112 | tf_op jit(solution)/shard_map/reduce_scatter | solution.py:106
  485.3 210.0 %reduce-scatter.4.cloned.1.call-start = ((), (), s32[]{:S(2)}) async-start(), calls=%async_computation.5 | async-start | bytes 4718592 | tf_op jit(solution)/shard_map/reduce_scatter | solution.py:109
Sparse Core Ops, SparseCore 0:
  10.3 57.8 all-gather.2
  70.6 51.1 all-gather.4
  257.6 81.4 all-reduce.2
  484.8 60.0 reduce-scatter.7
  547.1 61.0 reduce-scatter.5
  611.9 83.2 reduce-scatter.3

commit v2 on v1

--- a/solution.py
+++ b/solution.py
@@ -11,7 +11,11 @@
 
 
 def positions(token_index, block_order):
-    return block_order[token_index // BLK] * BLK + token_index % BLK
+    block_index = token_index // BLK
+    block_ids = jnp.arange(block_order.shape[0], dtype=jnp.int32)
+    matches = block_index[:, None] == block_ids[None, :]
+    start = jnp.sum(jnp.where(matches, block_order[None, :], 0), axis=1)
+    return start * BLK + token_index % BLK
 
 
 def partial_stats(scores, visible, weight_grad):
@@ -37,10 +41,15 @@
     r = lax.axis_index("row")
     c = lax.axis_index("col")
     local_rows = queries.shape[0]
-    query_all = lax.all_gather(queries, "row", axis=0, tiled=True)
-    grad_all = lax.all_gather(out_grad, "row", axis=0, tiled=True)
-    key_all = lax.all_gather(key_states, "col", axis=0, tiled=True)
-    value_all = lax.all_gather(value_states, "col", axis=0, tiled=True)
+    width = queries.shape[1]
+    pair_all = lax.all_gather(
+        jnp.concatenate([queries, out_grad], axis=1), "row", axis=0, tiled=True
+    )
+    query_all, grad_all = pair_all[:, :width], pair_all[:, width:]
+    kv_all = lax.all_gather(
+        jnp.concatenate([key_states, value_states], axis=1), "col", axis=0, tiled=True
+    )
+    key_all, value_all = kv_all[:, :HD], kv_all[:, HD:]
     q_total = query_all.shape[0]
     k_total = key_all.shape[0]
 
@@ -78,9 +87,11 @@
     (maxima, summed, weighted), _ = lax.scan(
         stats_pass, start, (key_blocks, value_blocks, kpos_blocks)
     )
-    top = lax.pmax(maxima, "row")
-    factor = jnp.exp(maxima - top)
-    summed, weighted = lax.psum((summed * factor, weighted * factor), "row")
+    gathered = lax.all_gather(jnp.stack([maxima, summed, weighted]), "row", axis=0)
+    top = jnp.max(gathered[:, 0], axis=0)
+    factor = jnp.exp(gathered[:, 0] - top[None])
+    summed = jnp.sum(gathered[:, 1] * factor, axis=0)
+    weighted = jnp.sum(gathered[:, 2] * factor, axis=0)
     logsum = top + jnp.log(summed)
     deltas = weighted / summed
 
@@ -101,10 +112,11 @@
         jnp.zeros((rows, HD), jnp.float32),
         (key_blocks, value_blocks, kpos_blocks),
     )
-    key_parts = key_parts.reshape(k_total, HD)
-    value_parts = value_parts.reshape(k_total, HD)
-    key_grad = lax.psum_scatter(key_parts, "col", scatter_dimension=0, tiled=True)
-    value_grad = lax.psum_scatter(value_parts, "col", scatter_dimension=0, tiled=True)
+    kv_parts = jnp.concatenate(
+        [key_parts.reshape(k_total, HD), value_parts.reshape(k_total, HD)], axis=1
+    )
+    kv_grad = lax.psum_scatter(kv_parts, "col", scatter_dimension=0, tiled=True)
+    key_grad, value_grad = kv_grad[:, :HD], kv_grad[:, HD:]
     query_acc = query_acc.reshape(q_total, H * HD)
     query_grad = lax.psum_scatter(query_acc, "row", scatter_dimension=0, tiled=True)
     return (

time: 705 us -> 566 us (0.80)
  waiting for transfers between devices: 329 us -> 245 us
  blocking collectives: 84.4 us -> 38 us
  local copies, waits for them, and re-layouts: 33.8 us -> 19.3 us
  other arithmetic: 37.4 us -> 44.5 us
    psum x1 -> x0, waiting for transfers between devices: 81.6 us -> none  [tile_grid(): summed, weighted = lax.psum((summed * factor, weighted * factor), 'row')]
    all_gather x2, waiting for transfers between devices: 43.5 us -> 103 us  [the longest x1 71.2 us: tile_grid(): lax.all_gather(jnp.concatenate([queries, out_grad], axis=1), 'row', axis=...]
    reduce_scatter x2 -> x1, waiting for transfers between devices: 117 us -> 57.8 us  [tile_grid(): kv_grad = lax.psum_scatter(kv_parts, 'col', scatter_dimension=0, tiled=True)]
    pmax x1 -> x0, blocking collectives: 38.1 us -> none  [tile_grid(): top = lax.pmax(maxima, 'row')]
    gather x2 -> x0, local copies, waits for them, and re-layouts: 20.1 us -> none  [positions(): return block_order[token_index // BLK] * BLK + token_index % BLK]
    all_gather x2 -> x1, blocking collectives: 46.3 us -> 38 us  [tile_grid(): lax.all_gather(jnp.stack([maxima, summed, weighted]), 'row', axis=0)]
    slice x0 -> x3, local copies, waits for them, and re-layouts: none -> 7.53 us  [the longest x1 3.99 us: tile_grid(): query_all, grad_all = (pair_all[:, :width], pair_all[:, width:])]
  transfers between devices with their start and end apart: 6 -> 4, of which waited for: 5 -> 4; matrix products, arithmetic and copies ran while one was open for 4% -> 3% of each run, Pallas kernels for 0% -> 0%
where the time goes in v2:
time: 566 us; the launch traced here: 565 us
  waiting for transfers between devices  245 us (43%)
  matrix products  203 us (36%)
  other arithmetic  44.5 us (8%)
  blocking collectives  38 us (7%)
  local copies, waits for them, and re-layouts  19.3 us (3%)
  between operations  13.9 us (2%)
    reduce_scatter x1, waiting for transfers between devices, tile_grid(): lax.psum_scatter(query_acc, 'row', scatter_dimension=0, tiled=True)  84.3 us
    all_gather x1, waiting for transfers between devices, tile_grid(): lax.all_gather(jnp.concatenate([queries, out_grad], axis=1), 'row', axis=...  71.2 us
    reduce_scatter x1, waiting for transfers between devices, tile_grid(): kv_grad = lax.psum_scatter(kv_parts, 'col', scatter_dimension=0, tiled=True)  57.8 us
    dot_general x4, matrix products, scores_of(): s = jnp.dot(qf, key_blk.T, preferred_element_type=jnp.float32) * scaling  51.4 us
    dot_general x2, matrix products, grad_pass(): dp = jnp.dot(gf, value_blk.T, preferred_element_type=jnp.float32)  42.9 us
    all_gather x1, blocking collectives, tile_grid(): lax.all_gather(jnp.stack([maxima, summed, weighted]), 'row', axis=0)  38 us
    dot_general x2, matrix products, stats_pass(): dp = jnp.dot(gf, value_blk.T, preferred_element_type=jnp.float32)  35.2 us
    all_gather x1, waiting for transfers between devices, tile_grid(): lax.all_gather(jnp.concatenate([key_states, value_states], axis=1), 'col'...  31.8 us
  transfers between devices with their start and end apart: 4, of which 4 were waited for; matrix products, arithmetic and copies ran while one was open for 3% of the time, Pallas kernels for 0%

profile of v2, /device:TPU:0, one launch (start us, length us, event | category | flops | bytes accessed | tf_op | source)
XLA Modules:
  0.0 564.9 jit_solution(5264457774797263037)
XLA Ops:
  8.7 1.9 pad_maximum_fusion.1
  13.3 31.8 %all-gather.5.cloned.1.call-done = bf16[2048,256]{1,0:T(8,128)(2,1)} async-done(((bf16[128,256]{1,0:T(8,128)(2,1)}), bf16[2048,256]{1,0:T(8,128)(2,1)}) %all-gather.5.cloned.1.call-update) | async-done | bytes 1048592 | tf_op jit(solution)/shard_map/all_gather | solution.py:49
  45.1 2.1 fusion.80
  47.2 71.2 %all-gather.7.cloned.1.call-done = bf16[1024,2048]{1,0:T(8,128)(2,1)} async-done(((bf16[128,2048]{1,0:T(8,128)(2,1)}), bf16[1024,2048]{1,0:T(8,128)(2,1)}) %all-gather.7.cloned.1.call-update) | async-done | bytes 4194320 | tf_op jit(solution)/shard_map/all_gather | solution.py:45
  118.4 4.0 fusion.78
  122.4 2.3 reshape.127
  124.7 2.8 reshape.125
  127.5 92.5 %while.30 = (s32[]{:T(128)}, f32[8192]{0:T(1024)S(1)}, f32[8192]{0:T(1024)S(1)}, f32[8192]{0:T(1024)S(1)}, s32[2,1024]{1,0:T(2,128)S(1)}, /*index=5*/bf16[2,1024...) while((s32[]{:T(128)}, f32[8192]{0:T(1024)S(1)}, ...), condition=%wide.region_6.7_spmd.clone, body=%wide.region_2.6_spmd.clone.sunk | while | flops 4437671936 | bytes 106225808 | solution.py:87
  128.0 12.6 %fusion.115 = (f32[8192]{0:T(1024)S(1)}, f32[1024,8192]{1,0:T(8,128)}) fusion(s32[8192]{0:T(1024)S(1)} %le.117, s32[1024]{0:T(1024)S(1)} %bitcast.146, bf16[8192,128]{1,0:T(8,128)(2,1)S(1)} %get-tuple-element.437, bf16[2,1024,128]{2,1,0:T(8,128)(2,1)S(1)} %get-tuple-element.436, s32[]{:T(128)S(6)} %copy.41), kind=kOutput, calls=%fused_computation.6.clone.1 | convolution fusion | flops 2181029888 | bytes 35983364 | tf_op jit(solution)/shard_map/while/body/eval_jaxpr/dot_general | solution.py:74
  140.6 17.6 %fusion.116 = f32[8192]{0:T(1024)S(1)} fusion(f32[1024,8192]{1,0:T(8,128)} %get-tuple-element.391, bf16[8192,128]{1,0:T(8,128)(2,1)} %get-tuple-element.439, f32[8192]{0:T(1024)S(1)} %get-tuple-element.392, s32[8192]{0:T(1024)S(1)} %le.117, s32[1024]{0:T(1024)S(1)} %bitcast.147, bf16[2,1024,128]{2,1,0:T(8,128)(2,1)} %get-tuple-element.438, s32[]{:T(128)S(6)} %copy.41), kind=kOutput, calls=%fused_computation.5.clone.1 | convolution fusion | flops 2206195712 | bytes 36016132 | tf_op jit(solution)/shard_map/while/body/eval_jaxpr/dot_general | solution.py:81
  158.2 15.4 %fusion.118 = f32[8192]{0:T(1024)S(1)} fusion(f32[1024,8192]{1,0:T(8,128)} %get-tuple-element.391, f32[8192]{0:T(1024)S(1)} %get-tuple-element.392, s32[8192]{0:T(1024)S(1)} %le.117, s32[1024]{0:T(1024)S(1)} %bitcast.148), kind=kLoop, calls=%fused_computation.7.clone.1 | loop fusion | flops 50323456 | bytes 33656832 | tf_op jit(solution)/shard_map/while/body/eval_jaxpr/reduce_sum | solution.py:24
  174.2 12.6 %fusion.115 = (f32[8192]{0:T(1024)S(1)}, f32[1024,8192]{1,0:T(8,128)}) fusion(s32[8192]{0:T(1024)S(1)} %le.117, s32[1024]{0:T(1024)S(1)} %bitcast.146, bf16[8192,128]{1,0:T(8,128)(2,1)S(1)} %get-tuple-element.437, bf16[2,1024,128]{2,1,0:T(8,128)(2,1)S(1)} %get-tuple-element.436, s32[]{:T(128)S(6)} %copy.41), kind=kOutput, calls=%fused_computation.6.clone.1 | convolution fusion | flops 2181029888 | bytes 35983364 | tf_op jit(solution)/shard_map/while/body/eval_jaxpr/dot_general | solution.py:74
  186.9 17.6 %fusion.116 = f32[8192]{0:T(1024)S(1)} fusion(f32[1024,8192]{1,0:T(8,128)} %get-tuple-element.391, bf16[8192,128]{1,0:T(8,128)(2,1)} %get-tuple-element.439, f32[8192]{0:T(1024)S(1)} %get-tuple-element.392, s32[8192]{0:T(1024)S(1)} %le.117, s32[1024]{0:T(1024)S(1)} %bitcast.147, bf16[2,1024,128]{2,1,0:T(8,128)(2,1)} %get-tuple-element.438, s32[]{:T(128)S(6)} %copy.41), kind=kOutput, calls=%fused_computation.5.clone.1 | convolution fusion | flops 2206195712 | bytes 36016132 | tf_op jit(solution)/shard_map/while/body/eval_jaxpr/dot_general | solution.py:81
  204.5 15.4 %fusion.118 = f32[8192]{0:T(1024)S(1)} fusion(f32[1024,8192]{1,0:T(8,128)} %get-tuple-element.391, f32[8192]{0:T(1024)S(1)} %get-tuple-element.392, s32[8192]{0:T(1024)S(1)} %le.117, s32[1024]{0:T(1024)S(1)} %bitcast.148), kind=kLoop, calls=%fused_computation.7.clone.1 | loop fusion | flops 50323456 | bytes 33656832 | tf_op jit(solution)/shard_map/while/body/eval_jaxpr/reduce_sum | solution.py:24
  220.1 38.0 %all-gather.1 = f32[8,3,8192]{2,1,0:T(4,128)S(1)} all-gather(f32[1,3,8192]{2,1,0:T(4,128)S(1)} %maximum_bitcast_fusion), channel_id=2, replica_groups=mesh['row'=8,'col'=16] {'row'}, dimensions={0}, use_global_device_ids=true | all-gather | bytes 884736 | tf_op jit(solution)/shard_map/all_gather | solution.py:90
  259.4 144.2 %while.31 = (s32[]{:T(128)}, f32[8192,128]{1,0:T(8,128)}, f32[2,1024,128]{2,1,0:T(8,128)}, f32[2,1024,128]{2,1,0:T(8,128)}, s32[2,1024]{1,0:T(2,128)S(1)}, /*ind...) while((s32[]{:T(128)}, f32[8192,128]{1,0:T(8,128)}, ...), condition=%wide.region_11.12_spmd.clone, body=%wide.region_10.11_spmd.clone.sunk | while | flops 10856955904 | bytes 180375776 | solution.py:110
  260.1 13.1 %fusion.130 = f32[1024,8192]{1,0:T(8,128)} fusion(bf16[8192,128]{1,0:T(8,128)(2,1)S(1)} %get-tuple-element.477, bf16[2,1024,128]{2,1,0:T(8,128)(2,1)S(1)} %get-tuple-element.476, s32[]{:T(128)S(6)} %copy.53), kind=kOutput, calls=%fused_computation.38.clone.1 | convolution fusion | flops 2147483648 | bytes 35913732 | tf_op jit(solution)/shard_map/while/body/eval_jaxpr/dot_general | solution.py:74
  273.2 15.1 %fusion.133 = f32[2,1024,128]{2,1,0:T(8,128)} fusion(f32[2,1024,128]{2,1,0:T(8,128)} %get-tuple-element.460, s32[]{:T(128)S(6)} %copy.53, bf16[8192,128]{1,0:T(8,128)(2,1)S(1)} %copy-done, f32[1024,8192]{1,0:T(8,128)} %fusion.130, f32[8192]{0:T(1024)S(1)} %get-tuple-element.478, s32[8192]{0:T(1024)S(1)} %le.124, s32[1024]{0:T(1024)S(1)} %bitcast.149), kind=kOutput, calls=%fused_computation.35.clone.1 | convolution fusion | flops 2197815296 | bytes 36245508 | tf_op jit(solution)/shard_map/while/body/eval_jaxpr/dot_general | solution.py:107
  288.3 21.4 %fusion.131 = bf16[8192,1024]{0,1:T(8,128)(2,1)} fusion(f32[1024,8192]{1,0:T(8,128)} %fusion.130, f32[8192]{0:T(1024)S(1)} %get-tuple-element.481, f32[8192]{0:T(1024)S(1)} %get-tuple-element.478, s32[8192]{0:T(1024)S(1)} %le.124, s32[1024]{0:T(1024)S(1)} %bitcast.150, bf16[8192,128]{1,0:T(8,128)(2,1)} %get-tuple-element.480, ...), kind=kOutput, calls=%fused_computation.28.clone.1 | convolution fusion | flops 2214592512 | bytes 52793348 | tf_op jit(solution)/shard_map/while/body/eval_jaxpr/dot_general | solution.py:102
  309.7 8.9 %fusion.132 = f32[2,1024,128]{2,1,0:T(8,128)} fusion(f32[2,1024,128]{2,1,0:T(8,128)} %get-tuple-element.459, s32[]{:T(128)S(6)} %copy.53, bf16[8192,1024]{0,1:T(8,128)(2,1)} %fusion.131, bf16[8192,128]{1,0:T(8,128)(2,1)S(1)} %get-tuple-element.477), kind=kOutput, calls=%fused_computation.33.clone.1 | convolution fusion | flops 2147483648 | bytes 19398660 | tf_op jit(solution)/shard_map/while/body/eval_jaxpr/dot_general | solution.py:106
  318.7 12.4 %convolution_add_fusion.2 = f32[8192,128]{1,0:T(8,128)} fusion(bf16[8192,1024]{0,1:T(8,128)(2,1)} %fusion.131, f32[8192,128]{1,0:T(8,128)} %get-tuple-element.458, pred[]{:T(512)S(6)} %compare.37, bf16[2,1024,128]{2,1,0:T(8,128)(2,1)S(1)} %get-tuple-element.476, s32[]{:T(128)S(6)} %copy.53), kind=kOutput, calls=%fused_computation.31.clone.1 | convolution fusion | flops 2149580800 | bytes 25427972 | tf_op jit(solution)/shard_map/while/body/eval_jaxpr/dot_general | solution.py:105
  331.5 13.1 %fusion.130 = f32[1024,8192]{1,0:T(8,128)} fusion(bf16[8192,128]{1,0:T(8,128)(2,1)S(1)} %get-tuple-element.477, bf16[2,1024,128]{2,1,0:T(8,128)(2,1)S(1)} %get-tuple-element.476, s32[]{:T(128)S(6)} %copy.53), kind=kOutput, calls=%fused_computation.38.clone.1 | convolution fusion | flops 2147483648 | bytes 35913732 | tf_op jit(solution)/shard_map/while/body/eval_jaxpr/dot_general | solution.py:74
  344.6 15.1 %fusion.133 = f32[2,1024,128]{2,1,0:T(8,128)} fusion(f32[2,1024,128]{2,1,0:T(8,128)} %get-tuple-element.460, s32[]{:T(128)S(6)} %copy.53, bf16[8192,128]{1,0:T(8,128)(2,1)S(1)} %copy-done, f32[1024,8192]{1,0:T(8,128)} %fusion.130, f32[8192]{0:T(1024)S(1)} %get-tuple-element.478, s32[8192]{0:T(1024)S(1)} %le.124, s32[1024]{0:T(1024)S(1)} %bitcast.149), kind=kOutput, calls=%fused_computation.35.clone.1 | convolution fusion | flops 2197815296 | bytes 36245508 | tf_op jit(solution)/shard_map/while/body/eval_jaxpr/dot_general | solution.py:107
  359.7 21.4 %fusion.131 = bf16[8192,1024]{0,1:T(8,128)(2,1)} fusion(f32[1024,8192]{1,0:T(8,128)} %fusion.130, f32[8192]{0:T(1024)S(1)} %get-tuple-element.481, f32[8192]{0:T(1024)S(1)} %get-tuple-element.478, s32[8192]{0:T(1024)S(1)} %le.124, s32[1024]{0:T(1024)S(1)} %bitcast.150, bf16[8192,128]{1,0:T(8,128)(2,1)} %get-tuple-element.480, ...), kind=kOutput, calls=%fused_computation.28.clone.1 | convolution fusion | flops 2214592512 | bytes 52793348 | tf_op jit(solution)/shard_map/while/body/eval_jaxpr/dot_general | solution.py:102
  381.1 8.9 %fusion.132 = f32[2,1024,128]{2,1,0:T(8,128)} fusion(f32[2,1024,128]{2,1,0:T(8,128)} %get-tuple-element.459, s32[]{:T(128)S(6)} %copy.53, bf16[8192,1024]{0,1:T(8,128)(2,1)} %fusion.131, bf16[8192,128]{1,0:T(8,128)(2,1)S(1)} %get-tuple-element.477), kind=kOutput, calls=%fused_computation.33.clone.1 | convolution fusion | flops 2147483648 | bytes 19398660 | tf_op jit(solution)/shard_map/while/body/eval_jaxpr/dot_general | solution.py:106
  390.0 13.6 %convolution_add_fusion.2 = f32[8192,128]{1,0:T(8,128)} fusion(bf16[8192,1024]{0,1:T(8,128)(2,1)} %fusion.131, f32[8192,128]{1,0:T(8,128)} %get-tuple-element.458, pred[]{:T(512)S(6)} %compare.37, bf16[2,1024,128]{2,1,0:T(8,128)(2,1)S(1)} %get-tuple-element.476, s32[]{:T(128)S(6)} %copy.53), kind=kOutput, calls=%fused_computation.31.clone.1 | convolution fusion | flops 2149580800 | bytes 25427972 | tf_op jit(solution)/shard_map/while/body/eval_jaxpr/dot_general | solution.py:105
  403.6 3.0 pad_maximum_fusion
  406.7 4.9 reshape.128
  411.6 57.8 %reduce-scatter.5.cloned.1.call-done = f32[128,256]{1,0:T(8,128)} async-done(((f32[2048,256]{1,0:T(8,128)}), f32[128,256]{1,0:T(8,128)}) %reduce-scatter.5.cloned.1.call-update) | async-done | bytes 131088 | tf_op jit(solution)/shard_map/reduce_scatter | solution.py:118
  470.8 1.5 fusion.47
  472.3 84.3 %reduce-scatter.3.cloned.1.call-done = f32[128,1024]{1,0:T(8,128)} async-done(((f32[1024,1024]{1,0:T(8,128)}), f32[128,1024]{1,0:T(8,128)}) %reduce-scatter.3.cloned.1.call-update) | async-done | bytes 524304 | tf_op jit(solution)/shard_map/reduce_scatter | solution.py:121
  556.6 1.8 multiply_convert_fusion
  (54 shorter events, 9.0 us)
Async XLA Ops:
  7.2 38.0 %all-gather.5.cloned.1.call-start = ((), (), s32[]{:S(2)}) async-start(), calls=%async_computation.2 | async-start | bytes 1114112 | tf_op jit(solution)/shard_map/all_gather | solution.py:49
  8.6 109.8 %all-gather.7.cloned.1.call-start = ((), (), s32[]{:S(2)}) async-start(), calls=%async_computation.3 | async-start | bytes 4718592 | tf_op jit(solution)/shard_map/all_gather | solution.py:45
  10.6 458.8 %reduce-scatter.5.cloned.1.call-start = ((), (), s32[]{:S(2)}) async-start(), calls=%async_computation.5 | async-start | bytes 2228224 | tf_op jit(solution)/shard_map/reduce_scatter | solution.py:118
  260.1 13.1 %copy-start = (bf16[8192,128]{1,0:T(8,128)(2,1)S(1)}, bf16[8192,128]{1,0:T(8,128)(2,1)}, u32[]{:S(2)}) copy-start(bf16[8192,128]{1,0:T(8,128)(2,1)} %get-tuple-element.480) | copy-start | bytes 6291460 | tf_op jit(solution)/shard_map/while
  273.2 15.1 %copy-start.1 = (bf16[2,1024,128]{2,1,0:T(8,128)(2,1)S(1)}, bf16[2,1024,128]{2,1,0:T(8,128)(2,1)}, u32[]{:S(2)}) copy-start(bf16[2,1024,128]{2,1,0:T(8,128)(2,1)} %get-tuple-element.479) | copy-start | bytes 1572868 | tf_op jit(solution)/shard_map/while
  331.5 13.1 %copy-start = (bf16[8192,128]{1,0:T(8,128)(2,1)S(1)}, bf16[8192,128]{1,0:T(8,128)(2,1)}, u32[]{:S(2)}) copy-start(bf16[8192,128]{1,0:T(8,128)(2,1)} %get-tuple-element.480) | copy-start | bytes 6291460 | tf_op jit(solution)/shard_map/while
  344.6 15.1 %copy-start.1 = (bf16[2,1024,128]{2,1,0:T(8,128)(2,1)S(1)}, bf16[2,1024,128]{2,1,0:T(8,128)(2,1)}, u32[]{:S(2)}) copy-start(bf16[2,1024,128]{2,1,0:T(8,128)(2,1)} %get-tuple-element.479) | copy-start | bytes 1572868 | tf_op jit(solution)/shard_map/while
  406.6 149.9 %reduce-scatter.3.cloned.1.call-start = ((), (), s32[]{:S(2)}) async-start(), calls=%async_computation.4 | async-start | bytes 4718592 | tf_op jit(solution)/shard_map/reduce_scatter | solution.py:121
Sparse Core Ops, SparseCore 0:
  10.2 34.8 all-gather.4
  47.5 70.8 all-gather.6
  406.7 62.5 reduce-scatter.4
  473.0 83.4 reduce-scatter.2
